TPU v7x, 512 devices: a whole 4x4x16 slice. The times are simulated.
512 devices in a mesh: gx: 32 (over z, core), gy: 4 (over x), gz: 4 (over y).
Axes of the slice: x: 4, y: 4, z: 16, core: 2. Of those that a mesh axis runs over, the one named last changes fastest.
Arguments:
- adjoint_final: float32 [16, 512, 512], P('gz', 'gx', 'gy'), may hold values from -6 to 6
- conductivity: float32 [3, 16, 512, 512], P(None, 'gz', 'gx', 'gy'), may hold values from 0.05 to 1
- step_ratio: float32 [16, 512, 512], P('gz', 'gx', 'gy'), may hold values from 0.04 to 0.16
- refine_rate: float32 [16, 512, 512], P('gz', 'gx', 'gy'), may hold values from 0.05 to 0.24
- residual: float32 [4, 8192], P(None, ('gx', 'gy')), may hold values from -6 to 6
- sensor_tile: int32 [8192], P(('gx', 'gy')), may hold values from 0 to 127, as said below
- sensor_cell: int32 [8192], P(('gx', 'gy')), may hold values from 0 to 32767
- substeps: int32 [32, 4], replicated, may hold values from 1 to 6, as said below
Outputs:
- adjoint_start: float32 [16, 512, 512], P('gz', 'gx', 'gy')
- sensitivity: float32 [16, 512, 512], P('gz', 'gx', 'gy')
Inputs may be any that keep to these rules, and one draw needn't show every extreme that they name: `sensor_tile`: tiles are numbered ix * 4 + iy. Among the 64 sensors of each aligned block at most 4 name one tile, and in every block some tile is named by exactly 4 of them. `substeps`: some tile takes 6 sub-steps in every draw.
All inputs are finite; a program needn't handle non-finite values.
Results may differ from a plain program's by a relative error of at most 0.000079.
Values sent between devices are 32-bit elements; how exact they have to be, the bound alone decides.
No kernel may reach another device: no remote copies, remote signals or barrier semaphores. Data moves between devices by JAX's collectives and lax.ppermute only.
A program may use at most 64 MiB of HBM per device.

v0:
```python
import jax
import jax.numpy as jnp
from jax import lax
from jax.sharding import PartitionSpec as P


def with_halo(cells, sides, width):
    for axis, dim in sides:
        count = lax.axis_size(axis)
        ends = count - 1
        head = lax.slice_in_dim(cells, 0, width, axis=dim)
        tail = lax.slice_in_dim(cells, cells.shape[dim] - width, cells.shape[dim], axis=dim)
        cells = jnp.concatenate(
            [
                lax.ppermute(tail, axis, [(i, (i + 1) % count) for i in range(ends)]),
                cells,
                lax.ppermute(head, axis, [((i + 1) % count, i) for i in range(ends)]),
            ],
            axis=dim,
        )
    return cells


def harmonic(first, second):
    return 2.0 * first * second / (first + second)


def lateral(field):
    down_diff = field[:, 1:, :] - field[:, :-1, :]
    side_diff = field[:, :, 1:] - field[:, :, :-1]
    rows_part = jnp.pad(down_diff, ((0, 0), (0, 1), (0, 0))) - jnp.pad(
        down_diff, ((0, 0), (1, 0), (0, 0))
    )
    cols_part = jnp.pad(side_diff, ((0, 0), (0, 0), (0, 1))) - jnp.pad(
        side_diff, ((0, 0), (0, 0), (1, 0))
    )
    return rows_part + cols_part


def refine(field, rates, count):

    def one_turn(turn, state):
        return state + lateral(rates * state)

    return lax.fori_loop(jnp.int32(0), count, one_turn, field)


def body(
    adjoint_final,
    conductivity,
    step_ratio,
    refine_rate,
    residual,
    sensor_tile,
    sensor_cell,
    substeps,
):
    layers, rows, cols = adjoint_final.shape
    steps = residual.shape[0]
    cells = layers * rows * cols
    row_dev = lax.axis_index("gx")
    col_dev = lax.axis_index("gy")
    layer_dev = lax.axis_index("gz")
    my_tile = row_dev * lax.axis_size("gy") + col_dev
    offset = layer_dev * cells
    padded = with_halo(conductivity, (("gx", 2), ("gy", 3), ("gz", 1)), 1)
    row_up = harmonic(conductivity[0], padded[0, 1:-1, 2:, 1:-1])
    row_down = harmonic(conductivity[0], padded[0, 1:-1, :-2, 1:-1])
    col_up = harmonic(conductivity[1], padded[1, 1:-1, 1:-1, 2:])
    col_down = harmonic(conductivity[1], padded[1, 1:-1, 1:-1, :-2])
    layer_up = harmonic(conductivity[2], padded[2, 2:, 1:-1, 1:-1])
    layer_down = harmonic(conductivity[2], padded[2, :-2, 1:-1, 1:-1])
    got_res, got_tile, got_cell = (
        lax.all_gather(residual, ("gx", "gy"), axis=1, tiled=True),
        lax.all_gather(sensor_tile.astype(jnp.float32), ("gx", "gy"), axis=0, tiled=True),
        lax.all_gather(sensor_cell.astype(jnp.float32), ("gx", "gy"), axis=0, tiled=True),
    )
    local_cell = got_cell.astype(jnp.int32) - offset
    keep = (got_tile.astype(jnp.int32) == my_tile) & (local_cell >= 0) & (local_cell < cells)
    index_of = jnp.where(keep, local_cell, 0)
    values_all = jnp.where(keep[None, :], got_res, 0.0)
    source = jnp.zeros((steps, cells), jnp.float32).at[:, index_of].add(values_all)
    my_count = substeps[row_dev, col_dev]
    adjoint = adjoint_final
    sensitivity = jnp.zeros_like(adjoint_final)
    for step_index in range(steps - 1, -1, -1):
        adjoint = adjoint + source[step_index].reshape(layers, rows, cols)
        weighted = step_ratio * adjoint
        wpad = with_halo(weighted, (("gx", 1), ("gy", 2), ("gz", 0)), 1)
        adjoint = adjoint + (
            row_up * (wpad[1:-1, 2:, 1:-1] - weighted)
            + row_down * (wpad[1:-1, :-2, 1:-1] - weighted)
            + col_up * (wpad[1:-1, 1:-1, 2:] - weighted)
            + col_down * (wpad[1:-1, 1:-1, :-2] - weighted)
            + layer_up * (wpad[2:, 1:-1, 1:-1] - weighted)
            + layer_down * (wpad[:-2, 1:-1, 1:-1] - weighted)
        )
        adjoint = refine(adjoint, refine_rate, my_count)
        sensitivity = sensitivity + step_ratio * adjoint
    return (adjoint, sensitivity)


def solution(mesh):
    return jax.shard_map(
        body,
        mesh=mesh,
        in_specs=(
            P("gz", "gx", "gy"),
            P(None, "gz", "gx", "gy"),
            P("gz", "gx", "gy"),
            P("gz", "gx", "gy"),
            P(None, ("gx", "gy")),
            P(("gx", "gy")),
            P(("gx", "gy")),
            P(),
        ),
        out_specs=(P("gz", "gx", "gy"), P("gz", "gx", "gy")),
        check_vma=False,
    )
```

profile of v0, /device:TPU:154, one launch (start us, length us, event | category | flops | bytes accessed | tf_op | source)
XLA Modules:
  0.0 543.7 jit_solution(5901369545518691948)
XLA Ops:
  8.0 1.9 collective-permute-start
  10.0 2.4 collective-permute-start.2
  16.5 174.7 %all-gather = f32[128,64,4]{1,2,0:T(4,128)S(1)} all-gather(f32[1,64,4]{1,2,0:T(4,128)} %bitcast.87), channel_id=1, replica_groups=mesh['gx'=32,'gy'=4,'gz'=4] {'gx','gy'}, dimensions={0}, use_global_device_ids=true | all-gather | bytes 132096 | tf_op jit(solution)/shard_map/all_gather | solution.py:74
  192.5 2.8 collective-permute-start.4
  195.3 3.0 collective-permute-start.6
  198.3 133.8 %all-reduce.21.cloned.1.call-done = (f32[8192]{0:T(1024)}, f32[8192]{0:T(1024)}) async-done(((f32[8192]{0:T(1024)}, f32[8192]{0:T(1024)}), (f32[8192]{0:T(1024)}, f32[8192]{0:T(1024)})) %all-reduce.21.cloned.1.call-update) | async-done | bytes 65552
  333.0 2.7 copy.13
  335.6 59.4 %scatter_custom_fusion = f32[4,8192]{0,1:T(8,128)} fusion(s32[8192]{0:T(1024)S(1)} %get-tuple-element.283, f32[8192,4]{1,0:T(8,128)} %copy.13, f32[]{:T(128)} %constant.63.clone.1), kind=kCustom, calls=%fused_computation.17 | custom fusion | flops 32768 | bytes 131584 | tf_op jit(solution)/shard_map/scatter-add | solution.py:82
  395.1 14.0 %slice_reduce_fusion = (f32[8192]{0:T(1024)S(1)}, f32[8192]{0:T(1024)S(1)}, f32[8192]{0:T(1024)S(1)}, f32[8192]{0:T(1024)S(1)}) fusion(f32[4,8192]{0,1:T(8,128)} %scatter_custom_fusion), kind=kLoop, calls=%fused_computation.13 | loop fusion | bytes 262144 | tf_op jit(solution)/shard_map/slice | solution.py:87
  409.1 3.7 collective-permute-start.1
  412.8 1.9 collective-permute-start.3
  414.9 4.0 collective-permute-done.3
  419.0 2.5 collective-permute-start.5
  421.5 3.3 collective-permute-start.7
  424.8 1.3 collective-permute-start.10
  426.1 4.5 collective-permute-start.8
  430.8 1.3 collective-permute-start.11
  432.1 4.5 collective-permute-start.9
  436.7 1.3 dynamic_slice.3
  438.4 5.6 %while.48 = (s32[]{:T(128)}, f32[4,16,128]{2,1,0:T(8,128)S(1)}, s32[]{:T(128)}, f32[4,16,128]{2,1,0:T(8,128)S(1)}, s32[]{:T(128)}) while((s32[]{:T(128)}, f32[4,16,128]{2,1,0:T(8,128)S(1)}, s32[]{:T(128)}, f32[4,16,128]{2,1,0:T(8,128)S(1)}, s32[]{:T(128)}) %tuple.137), condition=%wide.region_2.3_spmd, body=%wide.region_1.2_spmd.sunk | while | flops 56770 | bytes 416829 | solution.py:45
  444.0 1.9 collective-permute-start.12
  445.9 2.4 collective-permute-start.13
  448.4 3.7 collective-permute-done.13
  452.1 1.9 collective-permute-start.14
  454.1 3.9 collective-permute-start.15
  458.1 1.9 collective-permute-done.15
  460.1 4.2 collective-permute-start.16
  464.4 1.3 collective-permute-start.17
  465.9 4.2 collective-permute-done.17
  470.2 5.6 %while.49 = (s32[]{:T(128)}, f32[4,16,128]{2,1,0:T(8,128)S(1)}, s32[]{:T(128)}, f32[4,16,128]{2,1,0:T(8,128)S(1)}, s32[]{:T(128)}) while((s32[]{:T(128)}, f32[4,16,128]{2,1,0:T(8,128)S(1)}, s32[]{:T(128)}, f32[4,16,128]{2,1,0:T(8,128)S(1)}, s32[]{:T(128)}) %tuple.138), condition=%wide.region_4.5_spmd, body=%wide.region_3.4_spmd.sunk | while | flops 56770 | bytes 416829 | solution.py:45
  475.8 1.9 collective-permute-start.18
  477.8 2.4 collective-permute-start.19
  480.2 3.7 collective-permute-done.19
  484.0 1.9 collective-permute-start.20
  485.9 3.9 collective-permute-start.21
  490.0 1.9 collective-permute-done.21
  492.0 2.7 collective-permute-start.22
  496.2 4.2 collective-permute-done.23
  500.6 5.6 %while.50 = (s32[]{:T(128)}, f32[4,16,128]{2,1,0:T(8,128)S(1)}, s32[]{:T(128)}, f32[4,16,128]{2,1,0:T(8,128)S(1)}, s32[]{:T(128)}) while((s32[]{:T(128)}, f32[4,16,128]{2,1,0:T(8,128)S(1)}, s32[]{:T(128)}, f32[4,16,128]{2,1,0:T(8,128)S(1)}, s32[]{:T(128)}) %tuple.139), condition=%wide.region_6.7_spmd, body=%wide.region_5.6_spmd.sunk | while | flops 56770 | bytes 416829 | solution.py:45
  506.2 1.9 collective-permute-start.24
  508.1 2.4 collective-permute-start.25
  510.5 3.7 collective-permute-done.25
  514.3 1.9 collective-permute-start.26
  516.2 3.9 collective-permute-start.27
  520.3 1.9 collective-permute-done.27
  522.3 2.4 collective-permute-start.28
  526.2 4.2 collective-permute-done.29
  530.6 5.6 %while.51 = (s32[]{:T(128)}, f32[4,16,128]{2,1,0:T(8,128)S(1)}, s32[]{:T(128)}, f32[4,16,128]{2,1,0:T(8,128)S(1)}, s32[]{:T(128)}) while((s32[]{:T(128)}, f32[4,16,128]{2,1,0:T(8,128)S(1)}, s32[]{:T(128)}, f32[4,16,128]{2,1,0:T(8,128)S(1)}, s32[]{:T(128)}) %tuple.140), condition=%wide.region_8.9_spmd, body=%wide.region_7.8_spmd.sunk | while | flops 56770 | bytes 416829 | solution.py:45
  (172 shorter events, 16.4 us)
Async XLA Ops:
  7.2 325.0 %all-reduce.21.cloned.1.call-start = ((), (), s32[]{:S(2)}) async-start(), calls=%async_computation | async-start | bytes 131072
  8.0 183.4 %collective-permute-start = (f32[3,4,1,128]{3,2,1,0:T(1,128)S(1)}, f32[3,4,1,128]{3,2,1,0:T(1,128)S(1)}, u32[]{:S(2)}, u32[]{:S(2)}) collective-permute-start(f32[3,4,1,128]{3,2,1,0:T(1,128)S(1)} %get-tuple-element.298), channel_id=1, source_target_pairs={{16,0},{32,16},{48,32},{64,48},{80,64},{96,80},{112,96},{128,112},... | collective-permute-start | bytes 18440 | tf_op jit(solution)/shard_map/ppermute | solution.py:17
  10.0 181.4 %collective-permute-start.2 = (f32[3,4,1,128]{3,2,1,0:T(1,128)S(1)}, f32[3,4,1,128]{3,2,1,0:T(1,128)S(1)}, u32[]{:S(2)}, u32[]{:S(2)}) collective-permute-start(f32[3,4,1,128]{3,2,1,0:T(1,128)S(1)} %get-tuple-element.297), channel_id=1, source_target_pairs={{0,16},{16,32},{32,48},{48,64},{64,80},{80,96},{96,112},{112,128},... | collective-permute-start | bytes 18440 | tf_op jit(solution)/shard_map/ppermute | solution.py:15
  15.1 0.8 copy-start.5
  15.9 0.6 copy-start.4
  192.5 222.3 %collective-permute-start.4 = (f32[3,4,18,1]{3,2,1,0:T(8,128)S(1)}, f32[3,4,18,1]{3,2,1,0:T(8,128)S(1)}, u32[]{:S(2)}, u32[]{:S(2)}) collective-permute-start(f32[3,4,18,1]{3,2,1,0:T(8,128)S(1)} %get-tuple-element.288), channel_id=1, source_target_pairs={{4,0},{8,4},{12,8},{5,1},{9,5},{13,9},{6,2},{10,6},{14,10},{7,3},{... | collective-permute-start | bytes 2600 | tf_op jit(solution)/shard_map/ppermute | solution.py:17
  195.3 219.4 %collective-permute-start.6 = (f32[3,4,18,1]{3,2,1,0:T(8,128)S(1)}, f32[3,4,18,1]{3,2,1,0:T(8,128)S(1)}, u32[]{:S(2)}, u32[]{:S(2)}) collective-permute-start(f32[3,4,18,1]{3,2,1,0:T(8,128)S(1)} %get-tuple-element.287), channel_id=1, source_target_pairs={{0,4},{4,8},{8,12},{1,5},{5,9},{9,13},{2,6},{6,10},{10,14},{3,7},{... | collective-permute-start | bytes 2600 | tf_op jit(solution)/shard_map/ppermute | solution.py:15
  395.0 14.0 %copy-start.3 = (f32[4,16,128]{2,1,0:T(8,128)S(1)}, f32[4,16,128]{2,1,0:T(8,128)}, u32[]{:S(2)}) copy-start(f32[4,16,128]{2,1,0:T(8,128)} %param.18) | copy-start | bytes 98308
  395.0 14.0 %copy-start.6 = (f32[4,16,128]{2,1,0:T(8,128)S(1)}, f32[4,16,128]{2,1,0:T(8,128)}, u32[]{:S(2)}) copy-start(f32[4,16,128]{2,1,0:T(8,128)} %param.16) | copy-start | bytes 98308
  395.0 19.7 %copy-start.2 = (f32[3,4,16,128]{3,2,1,0:T(8,128)S(1)}, f32[3,4,16,128]{3,2,1,0:T(8,128)}, u32[]{:S(2)}) copy-start(f32[3,4,16,128]{3,2,1,0:T(8,128)} %param.17) | copy-start | bytes 294916
  395.0 43.3 %copy-start = (f32[4,16,128]{2,1,0:T(8,128)S(1)}, f32[4,16,128]{2,1,0:T(8,128)}, u32[]{:S(2)}) copy-start(f32[4,16,128]{2,1,0:T(8,128)} %param.19) | copy-start | bytes 98308
  409.1 5.8 %collective-permute-start.1 = (f32[4,1,128]{2,1,0:T(1,128)S(1)}, f32[4,1,128]{2,1,0:T(1,128)S(1)}, u32[]{:S(2)}, u32[]{:S(2)}) collective-permute-start(f32[4,1,128]{2,1,0:T(1,128)S(1)} %get-tuple-element.314), channel_id=1, source_target_pairs={{16,0},{32,16},{48,32},{64,48},{80,64},{96,80},{112,96},{128,112},... | collective-permute-start | bytes 6152 | tf_op jit(solution)/shard_map/ppermute | solution.py:17
  412.8 6.1 %collective-permute-start.3 = (f32[4,1,128]{2,1,0:T(1,128)S(1)}, f32[4,1,128]{2,1,0:T(1,128)S(1)}, u32[]{:S(2)}, u32[]{:S(2)}) collective-permute-start(f32[4,1,128]{2,1,0:T(1,128)S(1)} %get-tuple-element.313), channel_id=1, source_target_pairs={{0,16},{16,32},{32,48},{48,64},{64,80},{80,96},{96,112},{112,128},... | collective-permute-start | bytes 6152 | tf_op jit(solution)/shard_map/ppermute | solution.py:15
  419.0 11.7 %collective-permute-start.5 = (f32[4,18,1]{2,1,0:T(8,128)S(1)}, f32[4,18,1]{2,1,0:T(8,128)S(1)}, u32[]{:S(2)}, u32[]{:S(2)}) collective-permute-start(f32[4,18,1]{2,1,0:T(8,128)S(1)} %get-tuple-element.306), channel_id=1, source_target_pairs={{4,0},{8,4},{12,8},{5,1},{9,5},{13,9},{6,2},{10,6},{14,10},{7,3},{... | collective-permute-start | bytes 872 | tf_op jit(solution)/shard_map/ppermute | solution.py:17
  421.5 9.2 %collective-permute-start.7 = (f32[4,18,1]{2,1,0:T(8,128)S(1)}, f32[4,18,1]{2,1,0:T(8,128)S(1)}, u32[]{:S(2)}, u32[]{:S(2)}) collective-permute-start(f32[4,18,1]{2,1,0:T(8,128)S(1)} %get-tuple-element.305), channel_id=1, source_target_pairs={{0,4},{4,8},{8,12},{1,5},{5,9},{9,13},{2,6},{6,10},{10,14},{3,7},{... | collective-permute-start | bytes 872 | tf_op jit(solution)/shard_map/ppermute | solution.py:15
  424.8 13.2 %collective-permute-start.10 = (f32[3,1,18,130]{3,2,1,0:T(8,128)S(1)}, f32[3,1,18,130]{3,2,1,0:T(8,128)S(1)}, u32[]{:S(2)}, u32[]{:S(2)}) collective-permute-start(f32[3,1,18,130]{3,2,1,0:T(8,128)S(1)} %get-tuple-element.285), channel_id=1, source_target_pairs={{0,1},{1,2},{2,3},{4,5},{5,6},{6,7},{8,9},{9,10},{10,11},{12,13},{... | collective-permute-start | bytes 84248 | tf_op jit(solution)/shard_map/ppermute | solution.py:15
  426.1 11.9 %collective-permute-start.8 = (f32[3,1,18,130]{3,2,1,0:T(8,128)S(1)}, f32[3,1,18,130]{3,2,1,0:T(8,128)S(1)}, u32[]{:S(2)}, u32[]{:S(2)}) collective-permute-start(f32[3,1,18,130]{3,2,1,0:T(8,128)S(1)} %get-tuple-element.286), channel_id=1, source_target_pairs={{1,0},{2,1},{3,2},{5,4},{6,5},{7,6},{9,8},{10,9},{11,10},{13,12},{... | collective-permute-start | bytes 84248 | tf_op jit(solution)/shard_map/ppermute | solution.py:17
  430.8 7.2 %collective-permute-start.11 = (f32[1,18,130]{2,1,0:T(8,128)S(1)}, f32[1,18,130]{2,1,0:T(8,128)S(1)}, u32[]{:S(2)}, u32[]{:S(2)}) collective-permute-start(f32[1,18,130]{2,1,0:T(8,128)S(1)} %get-tuple-element.296), channel_id=1, source_target_pairs={{0,1},{1,2},{2,3},{4,5},{5,6},{6,7},{8,9},{9,10},{10,11},{12,13},{... | collective-permute-start | bytes 28088 | tf_op jit(solution)/shard_map/ppermute | solution.py:15
  432.1 6.1 %collective-permute-start.9 = (f32[1,18,130]{2,1,0:T(8,128)S(1)}, f32[1,18,130]{2,1,0:T(8,128)S(1)}, u32[]{:S(2)}, u32[]{:S(2)}) collective-permute-start(f32[1,18,130]{2,1,0:T(8,128)S(1)} %get-tuple-element.295), channel_id=1, source_target_pairs={{1,0},{2,1},{3,2},{5,4},{6,5},{7,6},{9,8},{10,9},{11,10},{13,12},{... | collective-permute-start | bytes 28088 | tf_op jit(solution)/shard_map/ppermute | solution.py:17
  444.0 4.3 collective-permute-start.12
  445.9 6.1 %collective-permute-start.13 = (f32[4,1,128]{2,1,0:T(1,128)S(1)}, f32[4,1,128]{2,1,0:T(1,128)S(1)}, u32[]{:S(2)}, u32[]{:S(2)}) collective-permute-start(f32[4,1,128]{2,1,0:T(1,128)S(1)} %get-tuple-element.311), channel_id=1, source_target_pairs={{0,16},{16,32},{32,48},{48,64},{64,80},{80,96},{96,112},{112,128},... | collective-permute-start | bytes 6152 | tf_op jit(solution)/shard_map/ppermute | solution.py:15
  452.1 6.0 %collective-permute-start.14 = (f32[4,18,1]{2,1,0:T(8,128)S(1)}, f32[4,18,1]{2,1,0:T(8,128)S(1)}, u32[]{:S(2)}, u32[]{:S(2)}) collective-permute-start(f32[4,18,1]{2,1,0:T(8,128)S(1)} %get-tuple-element.304), channel_id=1, source_target_pairs={{4,0},{8,4},{12,8},{5,1},{9,5},{13,9},{6,2},{10,6},{14,10},{7,3},{... | collective-permute-start | bytes 872 | tf_op jit(solution)/shard_map/ppermute | solution.py:17
  454.1 6.0 %collective-permute-start.15 = (f32[4,18,1]{2,1,0:T(8,128)S(1)}, f32[4,18,1]{2,1,0:T(8,128)S(1)}, u32[]{:S(2)}, u32[]{:S(2)}) collective-permute-start(f32[4,18,1]{2,1,0:T(8,128)S(1)} %get-tuple-element.303), channel_id=1, source_target_pairs={{0,4},{4,8},{8,12},{1,5},{5,9},{9,13},{2,6},{6,10},{10,14},{3,7},{... | collective-permute-start | bytes 872 | tf_op jit(solution)/shard_map/ppermute | solution.py:15
  460.1 5.7 %collective-permute-start.16 = (f32[1,18,130]{2,1,0:T(8,128)S(1)}, f32[1,18,130]{2,1,0:T(8,128)S(1)}, u32[]{:S(2)}, u32[]{:S(2)}) collective-permute-start(f32[1,18,130]{2,1,0:T(8,128)S(1)} %get-tuple-element.293), channel_id=1, source_target_pairs={{1,0},{2,1},{3,2},{5,4},{6,5},{7,6},{9,8},{10,9},{11,10},{13,12},{... | collective-permute-start | bytes 28088 | tf_op jit(solution)/shard_map/ppermute | solution.py:17
  464.4 5.7 %collective-permute-start.17 = (f32[1,18,130]{2,1,0:T(8,128)S(1)}, f32[1,18,130]{2,1,0:T(8,128)S(1)}, u32[]{:S(2)}, u32[]{:S(2)}) collective-permute-start(f32[1,18,130]{2,1,0:T(8,128)S(1)} %get-tuple-element.294), channel_id=1, source_target_pairs={{0,1},{1,2},{2,3},{4,5},{5,6},{6,7},{8,9},{9,10},{10,11},{12,13},{... | collective-permute-start | bytes 28088 | tf_op jit(solution)/shard_map/ppermute | solution.py:15
  475.8 4.3 collective-permute-start.18
  477.8 6.1 %collective-permute-start.19 = (f32[4,1,128]{2,1,0:T(1,128)S(1)}, f32[4,1,128]{2,1,0:T(1,128)S(1)}, u32[]{:S(2)}, u32[]{:S(2)}) collective-permute-start(f32[4,1,128]{2,1,0:T(1,128)S(1)} %get-tuple-element.309), channel_id=1, source_target_pairs={{0,16},{16,32},{32,48},{48,64},{64,80},{80,96},{96,112},{112,128},... | collective-permute-start | bytes 6152 | tf_op jit(solution)/shard_map/ppermute | solution.py:15
  484.0 6.0 %collective-permute-start.20 = (f32[4,18,1]{2,1,0:T(8,128)S(1)}, f32[4,18,1]{2,1,0:T(8,128)S(1)}, u32[]{:S(2)}, u32[]{:S(2)}) collective-permute-start(f32[4,18,1]{2,1,0:T(8,128)S(1)} %get-tuple-element.302), channel_id=1, source_target_pairs={{4,0},{8,4},{12,8},{5,1},{9,5},{13,9},{6,2},{10,6},{14,10},{7,3},{... | collective-permute-start | bytes 872 | tf_op jit(solution)/shard_map/ppermute | solution.py:17
  485.9 6.0 %collective-permute-start.21 = (f32[4,18,1]{2,1,0:T(8,128)S(1)}, f32[4,18,1]{2,1,0:T(8,128)S(1)}, u32[]{:S(2)}, u32[]{:S(2)}) collective-permute-start(f32[4,18,1]{2,1,0:T(8,128)S(1)} %get-tuple-element.301), channel_id=1, source_target_pairs={{0,4},{4,8},{8,12},{1,5},{5,9},{9,13},{2,6},{6,10},{10,14},{3,7},{... | collective-permute-start | bytes 872 | tf_op jit(solution)/shard_map/ppermute | solution.py:15
  492.0 4.2 collective-permute-start.22
  494.7 5.7 %collective-permute-start.23 = (f32[1,18,130]{2,1,0:T(8,128)S(1)}, f32[1,18,130]{2,1,0:T(8,128)S(1)}, u32[]{:S(2)}, u32[]{:S(2)}) collective-permute-start(f32[1,18,130]{2,1,0:T(8,128)S(1)} %get-tuple-element.292), channel_id=1, source_target_pairs={{0,1},{1,2},{2,3},{4,5},{5,6},{6,7},{8,9},{9,10},{10,11},{12,13},{... | collective-permute-start | bytes 28088 | tf_op jit(solution)/shard_map/ppermute | solution.py:15
  506.2 4.3 collective-permute-start.24
  508.1 6.1 %collective-permute-start.25 = (f32[4,1,128]{2,1,0:T(1,128)S(1)}, f32[4,1,128]{2,1,0:T(1,128)S(1)}, u32[]{:S(2)}, u32[]{:S(2)}) collective-permute-start(f32[4,1,128]{2,1,0:T(1,128)S(1)} %get-tuple-element.307), channel_id=1, source_target_pairs={{0,16},{16,32},{32,48},{48,64},{64,80},{80,96},{96,112},{112,128},... | collective-permute-start | bytes 6152 | tf_op jit(solution)/shard_map/ppermute | solution.py:15
  514.3 6.0 %collective-permute-start.26 = (f32[4,18,1]{2,1,0:T(8,128)S(1)}, f32[4,18,1]{2,1,0:T(8,128)S(1)}, u32[]{:S(2)}, u32[]{:S(2)}) collective-permute-start(f32[4,18,1]{2,1,0:T(8,128)S(1)} %get-tuple-element.300), channel_id=1, source_target_pairs={{4,0},{8,4},{12,8},{5,1},{9,5},{13,9},{6,2},{10,6},{14,10},{7,3},{... | collective-permute-start | bytes 872 | tf_op jit(solution)/shard_map/ppermute | solution.py:17
  516.2 6.0 %collective-permute-start.27 = (f32[4,18,1]{2,1,0:T(8,128)S(1)}, f32[4,18,1]{2,1,0:T(8,128)S(1)}, u32[]{:S(2)}, u32[]{:S(2)}) collective-permute-start(f32[4,18,1]{2,1,0:T(8,128)S(1)} %get-tuple-element.299), channel_id=1, source_target_pairs={{0,4},{4,8},{8,12},{1,5},{5,9},{9,13},{2,6},{6,10},{10,14},{3,7},{... | collective-permute-start | bytes 872 | tf_op jit(solution)/shard_map/ppermute | solution.py:15
  522.3 3.9 collective-permute-start.28
  524.7 5.7 %collective-permute-start.29 = (f32[1,18,130]{2,1,0:T(8,128)S(1)}, f32[1,18,130]{2,1,0:T(8,128)S(1)}, u32[]{:S(2)}, u32[]{:S(2)}) collective-permute-start(f32[1,18,130]{2,1,0:T(8,128)S(1)} %get-tuple-element.290), channel_id=1, source_target_pairs={{0,1},{1,2},{2,3},{4,5},{5,6},{6,7},{8,9},{9,10},{10,11},{12,13},{... | collective-permute-start | bytes 28088 | tf_op jit(solution)/shard_map/ppermute | solution.py:15
  536.2 0.6 copy-start.1
Sparse Core Ops, SparseCore 0:
  16.7 315.4 all-reduce.20
where the time goes:
time: 545 us; the launch traced here: 544 us
  blocking collectives  175 us (32%)
  waiting for transfers between devices  168 us (31%)
  starting transfers between devices  77 us (14%)
  other arithmetic  68.6 us (13%)
  local copies, waits for them, and re-layouts  21.3 us (4%)
  loops' own time  18.2 us (3%)
  between operations  15.3 us (3%)
    all_gather x1, blocking collectives, body(): lax.all_gather(residual, ('gx', 'gy'), axis=1, tiled=True)  175 us
    unnamed x2, waiting for transfers between devices  134 us
    scatter-add x1, other arithmetic, body(): jnp.zeros((steps, cells), jnp.float32).at[:, index_of].add(values_all)  59.4 us
    ppermute x15, starting transfers between devices, with_halo(): lax.ppermute(head, axis, [((i + 1) % count, i) for i in range(ends)])  40.9 us
    ppermute x15, starting transfers between devices, with_halo(): lax.ppermute(tail, axis, [(i, (i + 1) % count) for i in range(ends)])  36.1 us
    ppermute x15, waiting for transfers between devices, with_halo(): lax.ppermute(tail, axis, [(i, (i + 1) % count) for i in range(ends)])  33.5 us
    another operation x4, loops' own time, refine(): return lax.fori_loop(jnp.int32(0), count, one_turn, field)  18.2 us
    slice x1, local copies, waits for them, and re-layouts, body(): adjoint = adjoint + source[step_index].reshape(layers, rows, cols)  14 us
  transfers between devices with their start and end apart: 31, of which 18 were waited for; matrix products, arithmetic and copies ran while one was open for 15% of the time, Pallas kernels for 0%

commit v1 on v0

--- a/solution.py
+++ b/solution.py
@@ -2,6 +2,13 @@
 import jax.numpy as jnp
 from jax import lax
 from jax.sharding import PartitionSpec as P
+
+
+def exchange_gather(x, axis, along):
+    size = lax.axis_size(axis)
+    shards = jnp.stack([x for _ in range(size)])
+    shards = lax.all_to_all(shards, axis, split_axis=0, concat_axis=0)
+    return jnp.concatenate(shards, axis=along)
 
 
 def with_halo(cells, sides, width):
@@ -71,7 +78,7 @@
     layer_up = harmonic(conductivity[2], padded[2, 2:, 1:-1, 1:-1])
     layer_down = harmonic(conductivity[2], padded[2, :-2, 1:-1, 1:-1])
     got_res, got_tile, got_cell = (
-        lax.all_gather(residual, ("gx", "gy"), axis=1, tiled=True),
+        exchange_gather(residual, ("gx", "gy"), 1),
         lax.all_gather(sensor_tile.astype(jnp.float32), ("gx", "gy"), axis=0, tiled=True),
         lax.all_gather(sensor_cell.astype(jnp.float32), ("gx", "gy"), axis=0, tiled=True),
     )

time: 545 us -> 573 us (1.051)
  blocking collectives: 175 us -> 0 us
  waiting for transfers between devices: 168 us -> 342 us
  starting transfers between devices: 77 us -> 94.7 us
  other arithmetic: 68.6 us -> 77.3 us
    all_gather x1 -> x0, blocking collectives: 175 us -> none  [body(): lax.all_gather(residual, ('gx', 'gy'), axis=1, tiled=True)]
    unnamed x2, waiting for transfers between devices: 134 us -> 307 us
    all_to_all x0 -> x1, starting transfers between devices: none -> 17.7 us  [exchange_gather(): shards = lax.all_to_all(shards, axis, split_axis=0, concat_axis=0)]
    select_n x1, other arithmetic: 0.05 us -> 7.45 us  [body(): values_all = jnp.where(keep[None, :], got_res, 0.0)]
  transfers between devices with their start and end apart: 31 -> 32, of which waited for: 18 -> 18; matrix products, arithmetic and copies ran while one was open for 15% -> 16% of each run, Pallas kernels for 0% -> 0%
where the time goes in v1:
time: 573 us; the launch traced here: 572 us
  waiting for transfers between devices  342 us (60%)
  starting transfers between devices  94.7 us (17%)
  other arithmetic  77.3 us (13%)
  local copies, waits for them, and re-layouts  23.6 us (4%)
  loops' own time  18.6 us (3%)
  between operations  15.3 us (3%)
    unnamed x2, waiting for transfers between devices  307 us
    scatter-add x1, other arithmetic, body(): jnp.zeros((steps, cells), jnp.float32).at[:, index_of].add(values_all)  59.7 us
    ppermute x15, starting transfers between devices, with_halo(): lax.ppermute(head, axis, [((i + 1) % count, i) for i in range(ends)])  40.8 us
    ppermute x15, starting transfers between devices, with_halo(): lax.ppermute(tail, axis, [(i, (i + 1) % count) for i in range(ends)])  36.2 us
    ppermute x15, waiting for transfers between devices, with_halo(): lax.ppermute(tail, axis, [(i, (i + 1) % count) for i in range(ends)])  33.5 us
    another operation x4, loops' own time, refine(): return lax.fori_loop(jnp.int32(0), count, one_turn, field)  18.6 us
    all_to_all x1, starting transfers between devices, exchange_gather(): shards = lax.all_to_all(shards, axis, split_axis=0, concat_axis=0)  17.7 us
    slice x1, local copies, waits for them, and re-layouts, body(): adjoint = adjoint + source[step_index].reshape(layers, rows, cols)  14 us
  transfers between devices with their start and end apart: 32, of which 18 were waited for; matrix products, arithmetic and copies ran while one was open for 16% of the time, Pallas kernels for 0%

profile of v1, /device:TPU:154, one launch (start us, length us, event | category | flops | bytes accessed | tf_op | source)
XLA Modules:
  0.0 571.7 jit_solution(8727678282753523239)
XLA Ops:
  8.8 17.7 %all-to-all-start = ((f32[128,1,256]{2,1,0:T(1,128)}), f32[128,1,256]{2,1,0:T(1,128)S(1)}, u32[]{:S(2)}, u32[]{:S(2)}) async-start(f32[128,1,256]{2,1,0:T(1,128)} %reshape.40), calls=%async_computation | async-start | bytes 262144 | tf_op jit(solution)/shard_map/all_to_all | solution.py:10
  27.4 2.2 collective-permute-start
  29.6 2.2 collective-permute-start.2
  36.9 2.5 collective-permute-start.4
  39.4 3.4 collective-permute-start.6
  42.8 307.5 %all-reduce.21.cloned.1.call-done = (f32[8192]{0:T(1024)}, f32[8192]{0:T(1024)}) async-done(((f32[8192]{0:T(1024)}, f32[8192]{0:T(1024)}), (f32[8192]{0:T(1024)}, f32[8192]{0:T(1024)})) %all-reduce.21.cloned.1.call-update) | async-done | bytes 65552
  352.7 2.8 copy.12
  355.5 7.4 %bitcast_select_fusion = f32[4,8192]{0,1:T(8,128)} fusion(f32[4,128,64]{0,2,1:T(8,128)} %copy.12, pred[8192]{0:T(1024)(128)(4,1)S(1)} %get-tuple-element.284), kind=kLoop, calls=%fused_computation.19 | loop fusion | flops 32768 | bytes 270336 | tf_op jit(solution)/shard_map/jit(_where)/select_n | solution.py:88
  363.0 59.7 %scatter_custom_fusion = f32[4,8192]{0,1:T(8,128)} fusion(s32[8192]{0:T(1024)S(1)} %get-tuple-element.283, f32[4,8192]{0,1:T(8,128)} %bitcast_select_fusion, f32[]{:T(128)} %constant.63.clone.1), kind=kCustom, calls=%fused_computation.17 | custom fusion | flops 32768 | bytes 262148 | tf_op jit(solution)/shard_map/scatter-add | solution.py:89
  422.7 14.0 %slice_reduce_fusion = (f32[8192]{0:T(1024)S(1)}, f32[8192]{0:T(1024)S(1)}, f32[8192]{0:T(1024)S(1)}, f32[8192]{0:T(1024)S(1)}) fusion(f32[4,8192]{0,1:T(8,128)} %scatter_custom_fusion), kind=kLoop, calls=%fused_computation.13 | loop fusion | bytes 262144 | tf_op jit(solution)/shard_map/slice | solution.py:94
  436.7 3.7 collective-permute-start.1
  440.4 1.9 collective-permute-start.3
  442.5 4.0 collective-permute-done.3
  446.6 2.5 collective-permute-start.5
  449.2 3.3 collective-permute-start.7
  453.8 4.5 collective-permute-start.8
  459.7 4.5 collective-permute-start.9
  464.3 1.3 dynamic_slice.3
  466.0 5.7 while.48
  471.7 1.9 collective-permute-start.12
  473.6 2.4 collective-permute-start.13
  476.1 3.7 collective-permute-done.13
  479.8 1.9 collective-permute-start.14
  481.8 3.9 collective-permute-start.15
  485.8 1.9 collective-permute-done.15
  487.9 4.2 collective-permute-start.16
  493.6 4.2 collective-permute-done.17
  497.9 5.7 while.49
  503.6 1.9 collective-permute-start.18
  505.6 2.4 collective-permute-start.19
  508.0 3.7 collective-permute-done.19
  511.8 1.9 collective-permute-start.20
  513.7 3.9 collective-permute-start.21
  517.8 1.9 collective-permute-done.21
  519.8 2.7 collective-permute-start.22
  522.5 1.3 collective-permute-start.23
  524.0 4.2 collective-permute-done.23
  528.4 5.7 while.50
  534.1 1.9 collective-permute-start.24
  536.0 2.4 collective-permute-start.25
  538.4 3.7 collective-permute-done.25
  542.2 1.9 collective-permute-start.26
  544.1 3.9 collective-permute-start.27
  548.2 1.9 collective-permute-done.27
  550.2 2.4 collective-permute-start.28
  552.6 1.3 collective-permute-start.29
  554.1 4.2 collective-permute-done.29
  558.5 5.7 while.51
  (176 shorter events, 20.7 us)
Async XLA Ops:
  8.8 342.3 %all-to-all-start = ((f32[128,1,256]{2,1,0:T(1,128)}), f32[128,1,256]{2,1,0:T(1,128)S(1)}, u32[]{:S(2)}, u32[]{:S(2)}) async-start(f32[128,1,256]{2,1,0:T(1,128)} %reshape.40), calls=%async_computation | async-start | bytes 262144 | tf_op jit(solution)/shard_map/all_to_all | solution.py:10
  26.5 323.8 %all-reduce.21.cloned.1.call-start = ((), (), s32[]{:S(2)}) async-start(), calls=%async_computation.1 | async-start | bytes 131072
  27.4 8.5 %collective-permute-start = (f32[3,4,1,128]{3,2,1,0:T(1,128)S(1)}, f32[3,4,1,128]{3,2,1,0:T(1,128)S(1)}, u32[]{:S(2)}, u32[]{:S(2)}) collective-permute-start(f32[3,4,1,128]{3,2,1,0:T(1,128)S(1)} %get-tuple-element.298), channel_id=1, source_target_pairs={{16,0},{32,16},{48,32},{64,48},{80,64},{96,80},{112,96},{128,112},... | collective-permute-start | bytes 18440 | tf_op jit(solution)/shard_map/ppermute | solution.py:24
  29.6 6.3 %collective-permute-start.2 = (f32[3,4,1,128]{3,2,1,0:T(1,128)S(1)}, f32[3,4,1,128]{3,2,1,0:T(1,128)S(1)}, u32[]{:S(2)}, u32[]{:S(2)}) collective-permute-start(f32[3,4,1,128]{3,2,1,0:T(1,128)S(1)} %get-tuple-element.297), channel_id=1, source_target_pairs={{0,16},{16,32},{32,48},{48,64},{64,80},{80,96},{96,112},{112,128},... | collective-permute-start | bytes 18440 | tf_op jit(solution)/shard_map/ppermute | solution.py:22
  34.5 0.8 copy-start.5
  35.2 0.6 copy-start.4
  36.9 405.4 %collective-permute-start.4 = (f32[3,4,18,1]{3,2,1,0:T(8,128)S(1)}, f32[3,4,18,1]{3,2,1,0:T(8,128)S(1)}, u32[]{:S(2)}, u32[]{:S(2)}) collective-permute-start(f32[3,4,18,1]{3,2,1,0:T(8,128)S(1)} %get-tuple-element.288), channel_id=1, source_target_pairs={{4,0},{8,4},{12,8},{5,1},{9,5},{13,9},{6,2},{10,6},{14,10},{7,3},{... | collective-permute-start | bytes 2600 | tf_op jit(solution)/shard_map/ppermute | solution.py:24
  39.4 402.9 %collective-permute-start.6 = (f32[3,4,18,1]{3,2,1,0:T(8,128)S(1)}, f32[3,4,18,1]{3,2,1,0:T(8,128)S(1)}, u32[]{:S(2)}, u32[]{:S(2)}) collective-permute-start(f32[3,4,18,1]{3,2,1,0:T(8,128)S(1)} %get-tuple-element.287), channel_id=1, source_target_pairs={{0,4},{4,8},{8,12},{1,5},{5,9},{9,13},{2,6},{6,10},{10,14},{3,7},{... | collective-permute-start | bytes 2600 | tf_op jit(solution)/shard_map/ppermute | solution.py:22
  422.7 14.0 %copy-start.3 = (f32[4,16,128]{2,1,0:T(8,128)S(1)}, f32[4,16,128]{2,1,0:T(8,128)}, u32[]{:S(2)}) copy-start(f32[4,16,128]{2,1,0:T(8,128)} %param.18) | copy-start | bytes 98308
  422.7 14.0 %copy-start.6 = (f32[4,16,128]{2,1,0:T(8,128)S(1)}, f32[4,16,128]{2,1,0:T(8,128)}, u32[]{:S(2)}) copy-start(f32[4,16,128]{2,1,0:T(8,128)} %param.16) | copy-start | bytes 98308
  422.7 19.7 %copy-start.2 = (f32[3,4,16,128]{3,2,1,0:T(8,128)S(1)}, f32[3,4,16,128]{3,2,1,0:T(8,128)}, u32[]{:S(2)}) copy-start(f32[3,4,16,128]{3,2,1,0:T(8,128)} %param.17) | copy-start | bytes 294916
  422.7 43.3 %copy-start = (f32[4,16,128]{2,1,0:T(8,128)S(1)}, f32[4,16,128]{2,1,0:T(8,128)}, u32[]{:S(2)}) copy-start(f32[4,16,128]{2,1,0:T(8,128)} %param.19) | copy-start | bytes 98308
  436.7 5.8 %collective-permute-start.1 = (f32[4,1,128]{2,1,0:T(1,128)S(1)}, f32[4,1,128]{2,1,0:T(1,128)S(1)}, u32[]{:S(2)}, u32[]{:S(2)}) collective-permute-start(f32[4,1,128]{2,1,0:T(1,128)S(1)} %get-tuple-element.314), channel_id=1, source_target_pairs={{16,0},{32,16},{48,32},{64,48},{80,64},{96,80},{112,96},{128,112},... | collective-permute-start | bytes 6152 | tf_op jit(solution)/shard_map/ppermute | solution.py:24
  440.4 6.1 %collective-permute-start.3 = (f32[4,1,128]{2,1,0:T(1,128)S(1)}, f32[4,1,128]{2,1,0:T(1,128)S(1)}, u32[]{:S(2)}, u32[]{:S(2)}) collective-permute-start(f32[4,1,128]{2,1,0:T(1,128)S(1)} %get-tuple-element.313), channel_id=1, source_target_pairs={{0,16},{16,32},{32,48},{48,64},{64,80},{80,96},{96,112},{112,128},... | collective-permute-start | bytes 6152 | tf_op jit(solution)/shard_map/ppermute | solution.py:22
  446.6 11.7 %collective-permute-start.5 = (f32[4,18,1]{2,1,0:T(8,128)S(1)}, f32[4,18,1]{2,1,0:T(8,128)S(1)}, u32[]{:S(2)}, u32[]{:S(2)}) collective-permute-start(f32[4,18,1]{2,1,0:T(8,128)S(1)} %get-tuple-element.306), channel_id=1, source_target_pairs={{4,0},{8,4},{12,8},{5,1},{9,5},{13,9},{6,2},{10,6},{14,10},{7,3},{... | collective-permute-start | bytes 872 | tf_op jit(solution)/shard_map/ppermute | solution.py:24
  449.2 9.2 %collective-permute-start.7 = (f32[4,18,1]{2,1,0:T(8,128)S(1)}, f32[4,18,1]{2,1,0:T(8,128)S(1)}, u32[]{:S(2)}, u32[]{:S(2)}) collective-permute-start(f32[4,18,1]{2,1,0:T(8,128)S(1)} %get-tuple-element.305), channel_id=1, source_target_pairs={{0,4},{4,8},{8,12},{1,5},{5,9},{9,13},{2,6},{6,10},{10,14},{3,7},{... | collective-permute-start | bytes 872 | tf_op jit(solution)/shard_map/ppermute | solution.py:22
  452.5 13.1 %collective-permute-start.10 = (f32[3,1,18,130]{3,2,1,0:T(8,128)S(1)}, f32[3,1,18,130]{3,2,1,0:T(8,128)S(1)}, u32[]{:S(2)}, u32[]{:S(2)}) collective-permute-start(f32[3,1,18,130]{3,2,1,0:T(8,128)S(1)} %get-tuple-element.285), channel_id=1, source_target_pairs={{0,1},{1,2},{2,3},{4,5},{5,6},{6,7},{8,9},{9,10},{10,11},{12,13},{... | collective-permute-start | bytes 84248 | tf_op jit(solution)/shard_map/ppermute | solution.py:22
  453.8 11.8 %collective-permute-start.8 = (f32[3,1,18,130]{3,2,1,0:T(8,128)S(1)}, f32[3,1,18,130]{3,2,1,0:T(8,128)S(1)}, u32[]{:S(2)}, u32[]{:S(2)}) collective-permute-start(f32[3,1,18,130]{3,2,1,0:T(8,128)S(1)} %get-tuple-element.286), channel_id=1, source_target_pairs={{1,0},{2,1},{3,2},{5,4},{6,5},{7,6},{9,8},{10,9},{11,10},{13,12},{... | collective-permute-start | bytes 84248 | tf_op jit(solution)/shard_map/ppermute | solution.py:24
  458.4 7.2 %collective-permute-start.11 = (f32[1,18,130]{2,1,0:T(8,128)S(1)}, f32[1,18,130]{2,1,0:T(8,128)S(1)}, u32[]{:S(2)}, u32[]{:S(2)}) collective-permute-start(f32[1,18,130]{2,1,0:T(8,128)S(1)} %get-tuple-element.296), channel_id=1, source_target_pairs={{0,1},{1,2},{2,3},{4,5},{5,6},{6,7},{8,9},{9,10},{10,11},{12,13},{... | collective-permute-start | bytes 28088 | tf_op jit(solution)/shard_map/ppermute | solution.py:22
  459.7 6.1 %collective-permute-start.9 = (f32[1,18,130]{2,1,0:T(8,128)S(1)}, f32[1,18,130]{2,1,0:T(8,128)S(1)}, u32[]{:S(2)}, u32[]{:S(2)}) collective-permute-start(f32[1,18,130]{2,1,0:T(8,128)S(1)} %get-tuple-element.295), channel_id=1, source_target_pairs={{1,0},{2,1},{3,2},{5,4},{6,5},{7,6},{9,8},{10,9},{11,10},{13,12},{... | collective-permute-start | bytes 28088 | tf_op jit(solution)/shard_map/ppermute | solution.py:24
  471.7 4.3 collective-permute-start.12
  473.6 6.1 %collective-permute-start.13 = (f32[4,1,128]{2,1,0:T(1,128)S(1)}, f32[4,1,128]{2,1,0:T(1,128)S(1)}, u32[]{:S(2)}, u32[]{:S(2)}) collective-permute-start(f32[4,1,128]{2,1,0:T(1,128)S(1)} %get-tuple-element.311), channel_id=1, source_target_pairs={{0,16},{16,32},{32,48},{48,64},{64,80},{80,96},{96,112},{112,128},... | collective-permute-start | bytes 6152 | tf_op jit(solution)/shard_map/ppermute | solution.py:22
  479.8 6.0 %collective-permute-start.14 = (f32[4,18,1]{2,1,0:T(8,128)S(1)}, f32[4,18,1]{2,1,0:T(8,128)S(1)}, u32[]{:S(2)}, u32[]{:S(2)}) collective-permute-start(f32[4,18,1]{2,1,0:T(8,128)S(1)} %get-tuple-element.304), channel_id=1, source_target_pairs={{4,0},{8,4},{12,8},{5,1},{9,5},{13,9},{6,2},{10,6},{14,10},{7,3},{... | collective-permute-start | bytes 872 | tf_op jit(solution)/shard_map/ppermute | solution.py:24
  481.8 6.0 %collective-permute-start.15 = (f32[4,18,1]{2,1,0:T(8,128)S(1)}, f32[4,18,1]{2,1,0:T(8,128)S(1)}, u32[]{:S(2)}, u32[]{:S(2)}) collective-permute-start(f32[4,18,1]{2,1,0:T(8,128)S(1)} %get-tuple-element.303), channel_id=1, source_target_pairs={{0,4},{4,8},{8,12},{1,5},{5,9},{9,13},{2,6},{6,10},{10,14},{3,7},{... | collective-permute-start | bytes 872 | tf_op jit(solution)/shard_map/ppermute | solution.py:22
  487.9 5.7 %collective-permute-start.16 = (f32[1,18,130]{2,1,0:T(8,128)S(1)}, f32[1,18,130]{2,1,0:T(8,128)S(1)}, u32[]{:S(2)}, u32[]{:S(2)}) collective-permute-start(f32[1,18,130]{2,1,0:T(8,128)S(1)} %get-tuple-element.293), channel_id=1, source_target_pairs={{1,0},{2,1},{3,2},{5,4},{6,5},{7,6},{9,8},{10,9},{11,10},{13,12},{... | collective-permute-start | bytes 28088 | tf_op jit(solution)/shard_map/ppermute | solution.py:24
  492.1 5.7 %collective-permute-start.17 = (f32[1,18,130]{2,1,0:T(8,128)S(1)}, f32[1,18,130]{2,1,0:T(8,128)S(1)}, u32[]{:S(2)}, u32[]{:S(2)}) collective-permute-start(f32[1,18,130]{2,1,0:T(8,128)S(1)} %get-tuple-element.294), channel_id=1, source_target_pairs={{0,1},{1,2},{2,3},{4,5},{5,6},{6,7},{8,9},{9,10},{10,11},{12,13},{... | collective-permute-start | bytes 28088 | tf_op jit(solution)/shard_map/ppermute | solution.py:22
  503.6 4.3 collective-permute-start.18
  505.6 6.1 %collective-permute-start.19 = (f32[4,1,128]{2,1,0:T(1,128)S(1)}, f32[4,1,128]{2,1,0:T(1,128)S(1)}, u32[]{:S(2)}, u32[]{:S(2)}) collective-permute-start(f32[4,1,128]{2,1,0:T(1,128)S(1)} %get-tuple-element.309), channel_id=1, source_target_pairs={{0,16},{16,32},{32,48},{48,64},{64,80},{80,96},{96,112},{112,128},... | collective-permute-start | bytes 6152 | tf_op jit(solution)/shard_map/ppermute | solution.py:22
  511.8 6.0 %collective-permute-start.20 = (f32[4,18,1]{2,1,0:T(8,128)S(1)}, f32[4,18,1]{2,1,0:T(8,128)S(1)}, u32[]{:S(2)}, u32[]{:S(2)}) collective-permute-start(f32[4,18,1]{2,1,0:T(8,128)S(1)} %get-tuple-element.302), channel_id=1, source_target_pairs={{4,0},{8,4},{12,8},{5,1},{9,5},{13,9},{6,2},{10,6},{14,10},{7,3},{... | collective-permute-start | bytes 872 | tf_op jit(solution)/shard_map/ppermute | solution.py:24
  513.7 6.0 %collective-permute-start.21 = (f32[4,18,1]{2,1,0:T(8,128)S(1)}, f32[4,18,1]{2,1,0:T(8,128)S(1)}, u32[]{:S(2)}, u32[]{:S(2)}) collective-permute-start(f32[4,18,1]{2,1,0:T(8,128)S(1)} %get-tuple-element.301), channel_id=1, source_target_pairs={{0,4},{4,8},{8,12},{1,5},{5,9},{9,13},{2,6},{6,10},{10,14},{3,7},{... | collective-permute-start | bytes 872 | tf_op jit(solution)/shard_map/ppermute | solution.py:22
  519.8 4.2 collective-permute-start.22
  522.5 5.7 %collective-permute-start.23 = (f32[1,18,130]{2,1,0:T(8,128)S(1)}, f32[1,18,130]{2,1,0:T(8,128)S(1)}, u32[]{:S(2)}, u32[]{:S(2)}) collective-permute-start(f32[1,18,130]{2,1,0:T(8,128)S(1)} %get-tuple-element.292), channel_id=1, source_target_pairs={{0,1},{1,2},{2,3},{4,5},{5,6},{6,7},{8,9},{9,10},{10,11},{12,13},{... | collective-permute-start | bytes 28088 | tf_op jit(solution)/shard_map/ppermute | solution.py:22
  534.1 4.3 collective-permute-start.24
  536.0 6.1 %collective-permute-start.25 = (f32[4,1,128]{2,1,0:T(1,128)S(1)}, f32[4,1,128]{2,1,0:T(1,128)S(1)}, u32[]{:S(2)}, u32[]{:S(2)}) collective-permute-start(f32[4,1,128]{2,1,0:T(1,128)S(1)} %get-tuple-element.307), channel_id=1, source_target_pairs={{0,16},{16,32},{32,48},{48,64},{64,80},{80,96},{96,112},{112,128},... | collective-permute-start | bytes 6152 | tf_op jit(solution)/shard_map/ppermute | solution.py:22
  542.2 6.0 %collective-permute-start.26 = (f32[4,18,1]{2,1,0:T(8,128)S(1)}, f32[4,18,1]{2,1,0:T(8,128)S(1)}, u32[]{:S(2)}, u32[]{:S(2)}) collective-permute-start(f32[4,18,1]{2,1,0:T(8,128)S(1)} %get-tuple-element.300), channel_id=1, source_target_pairs={{4,0},{8,4},{12,8},{5,1},{9,5},{13,9},{6,2},{10,6},{14,10},{7,3},{... | collective-permute-start | bytes 872 | tf_op jit(solution)/shard_map/ppermute | solution.py:24
  544.1 6.0 %collective-permute-start.27 = (f32[4,18,1]{2,1,0:T(8,128)S(1)}, f32[4,18,1]{2,1,0:T(8,128)S(1)}, u32[]{:S(2)}, u32[]{:S(2)}) collective-permute-start(f32[4,18,1]{2,1,0:T(8,128)S(1)} %get-tuple-element.299), channel_id=1, source_target_pairs={{0,4},{4,8},{8,12},{1,5},{5,9},{9,13},{2,6},{6,10},{10,14},{3,7},{... | collective-permute-start | bytes 872 | tf_op jit(solution)/shard_map/ppermute | solution.py:22
  550.2 3.9 collective-permute-start.28
  552.6 5.7 %collective-permute-start.29 = (f32[1,18,130]{2,1,0:T(8,128)S(1)}, f32[1,18,130]{2,1,0:T(8,128)S(1)}, u32[]{:S(2)}, u32[]{:S(2)}) collective-permute-start(f32[1,18,130]{2,1,0:T(8,128)S(1)} %get-tuple-element.290), channel_id=1, source_target_pairs={{0,1},{1,2},{2,3},{4,5},{5,6},{6,7},{8,9},{9,10},{10,11},{12,13},{... | collective-permute-start | bytes 28088 | tf_op jit(solution)/shard_map/ppermute | solution.py:22
  564.2 0.6 copy-start.1
Sparse Core Ops, SparseCore 0:
  36.0 314.2 all-reduce.20
